TPU v7x, 256 devices: a whole 4x4x8 slice. The times are simulated.
256 devices in a mesh: fx: 32 (over z, x), fy: 8 (over y, core).
Axes of the slice: x: 4, y: 4, z: 8, core: 2. Of those that a mesh axis runs over, the one named last changes fastest.
Arguments:
- right_side: float32 [4096, 2048], P(('fx', 'fy'))
- coupling: float32 [4096, 11, 4096], P(('fx', 'fy')), may hold values from -0.109375 to 0.109375
- face_columns: int32 [4096, 11], P(('fx', 'fy')), may hold values from 0 to 31, as said below
- ghost_lists: int32 [1024, 4], P(('fx', 'fy')), may hold values from 0 to 15, as said below
Outputs:
- solution: float32 [4096, 2048], P(('fx', 'fy'))
- residual: float32 [4096, 2048], P(('fx', 'fy'))
Inputs may be any that keep to these rules, and one draw needn't show every extreme that they name: face_columns[f, 0] is f's own index within its block; entries 1 to 6 name other faces of the same block, all distinct and below 16; entries 7 to 10 are distinct and name received faces, 16 + d * 4 + g for the g-th face of group d of the extended list; every received slot of every block is named by some row of that block. `ghost_lists`: each row names 4 distinct faces of its block by local index.
All inputs are finite; a program needn't handle non-finite values.
Results may differ from a plain program's by a relative error of at most 0.0003.
Values sent between devices are 32-bit elements; how exact they have to be, the bound alone decides.
No kernel may reach another device: no remote copies, remote signals or barrier semaphores. Data moves between devices by JAX's collectives and lax.ppermute only.
A program may use at most 64 MiB of HBM per device.

v0:
```python
import jax
import jax.numpy as jnp
from jax import lax
from jax.sharding import PartitionSpec as P

DOF = 64
NRHS = 32
BLOCKS = 11
POWERS = 3


def from_behind(block, axis, distance):
    devices = range(lax.axis_size(axis))
    route = [(i - distance, i) for i in devices if i - distance in devices]
    return lax.ppermute(block, axis, route)


def receive_rows(field, ghost_lists):
    from_lower_x = from_behind(jnp.take(field, ghost_lists[1], axis=0), "fx", 1)
    from_upper_x = from_behind(jnp.take(field, ghost_lists[0], axis=0), "fx", -1)
    from_lower_y = from_behind(jnp.take(field, ghost_lists[3], axis=0), "fy", 1)
    from_upper_y = from_behind(jnp.take(field, ghost_lists[2], axis=0), "fy", -1)
    return jnp.concatenate([from_lower_x, from_upper_x, from_lower_y, from_upper_y], axis=0)


def contract(block_mats, picked):
    face_count = picked.shape[0]
    shaped = picked.reshape(face_count, picked.shape[1], DOF, NRHS)
    result = jnp.einsum("fkab,fkbr->far", block_mats, shaped, precision=lax.Precision.HIGHEST)
    return result.reshape(face_count, DOF * NRHS)


def solve_small(gram_total):
    count = NRHS
    row_ids = jnp.arange((POWERS + 1) * count)[:, None]
    col_ids = jnp.arange(POWERS * count)[None, :]
    shift_map = ((row_ids == col_ids) | (row_ids == col_ids + count)).astype(jnp.float32)
    first = (row_ids == jnp.arange(count)[None, :]).astype(jnp.float32)
    high = lax.Precision.HIGHEST
    normal_matrix = jnp.dot(
        shift_map.T, jnp.dot(gram_total, shift_map, precision=high), precision=high
    )
    right_terms = jnp.dot(shift_map.T, gram_total[:, :count], precision=high)
    factor = jnp.linalg.cholesky(normal_matrix)
    coeffs = jax.scipy.linalg.cho_solve((factor, True), right_terms)
    combo = first - jnp.dot(shift_map, coeffs, precision=high)
    return (coeffs, combo)


def on_device(right_side, coupling, face_columns, ghost_lists):
    face_count = right_side.shape[0]
    block_mats = coupling.reshape(face_count, BLOCKS, DOF, DOF)
    high = lax.Precision.HIGHEST

    def as_rows(field):
        return field.reshape(face_count * DOF, NRHS)

    fields = [right_side]
    for power_index in range(POWERS):
        power_field = fields[-1]
        received = receive_rows(power_field, ghost_lists)
        extended = jnp.concatenate([power_field, received], axis=0)
        fields.append(contract(block_mats, jnp.take(extended, face_columns, axis=0)))
    stacked = jnp.concatenate([as_rows(item) for item in fields], axis=1)
    local_gram = jnp.dot(stacked.T, stacked, precision=high, preferred_element_type=jnp.float32)
    gram_total = lax.psum(local_gram, ("fx", "fy"))
    coeffs, combo = solve_small(gram_total)
    solution = jnp.dot(stacked[:, : POWERS * NRHS], coeffs, precision=high)
    residual = jnp.dot(stacked, combo, precision=high)
    return (solution.reshape(face_count, DOF * NRHS), residual.reshape(face_count, DOF * NRHS))


def solution(mesh):
    placed = (
        P(("fx", "fy"), None),
        P(("fx", "fy"), None, None),
        P(("fx", "fy"), None),
        P(("fx", "fy"), None),
    )
    return jax.shard_map(
        on_device,
        mesh=mesh,
        in_specs=placed,
        out_specs=(P(("fx", "fy"), None), P(("fx", "fy"), None)),
        check_vma=False,
    )
```

profile of v0, /device:TPU:1, one launch (start us, length us, event | category | flops | bytes accessed | tf_op | source)
XLA Modules:
  0.0 415.1 jit_solution(4617153673329050650)
XLA Ops:
  8.1 1.5 gather_fusion
  9.6 3.9 collective-permute-start
  13.6 1.5 gather_fusion.1
  15.2 1.3 collective-permute-start.1
  16.5 1.5 gather_fusion.2
  18.0 4.0 collective-permute-start.2
  22.1 1.5 gather_fusion.3
  23.7 1.9 collective-permute-start.3
  27.1 5.7 %reshape.61 = f32[16,11,64,64]{3,2,0,1:T(8,128)} reshape(f32[16,11,4096]{2,0,1:T(8,128)} %param.9) | data formatting | bytes 5767168 | tf_op jit(solution)/shard_map/reshape | solution.py:52
  34.1 1.5 reshape.217
  35.6 1.8 broadcast_select_fusion.2
  37.4 3.6 reshape.245
  41.0 12.0 %fusion.6 = f32[16,64,32]{1,2,0:T(8,128)S(1)} fusion(f32[16,11,64,64]{3,2,0,1:T(8,128)} %reshape.61, f32[16,11,64,32]{3,2,1,0:T(8,128)} %reshape.245), kind=kOutput, calls=%fused_computation.21 | convolution fusion | flops 276824064 | bytes 4456448 | tf_op jit(solution)/shard_map/fkab,fkbr->far/dot_general | solution.py:29
  55.8 1.3 collective-permute-start.5
  57.2 3.6 collective-permute-start.6
  60.9 1.9 collective-permute-start.7
  62.9 5.1 %collective-permute-start.4 = (f32[4,2048]{1,0:T(4,128)S(1)}, f32[4,2048]{1,0:T(4,128)S(1)}, u32[]{:S(2)}, u32[]{:S(2)}) collective-permute-start(f32[4,2048]{1,0:T(4,128)S(1)} %broadcast_select_fusion.10), channel_id=1, source_target_pairs={{0,8},{8,16},{16,24},{24,32},{32,40},{40,48},{48,56},{56,64},{64,7... | collective-permute-start | bytes 98312 | tf_op jit(solution)/shard_map/ppermute | solution.py:15
  70.0 1.6 reshape.229
  71.7 3.2 broadcast_select_fusion.1
  74.9 5.2 %reshape.246 = f32[16,11,64,32]{3,2,1,0:T(8,128)} reshape(f32[16,11,2048]{2,1,0:T(8,128)} %broadcast_select_fusion.1) | data formatting | bytes 2883584 | tf_op jit(solution)/shard_map/reshape | solution.py:28
  80.1 12.0 %fusion.9 = f32[16,64,32]{1,2,0:T(8,128)S(1)} fusion(f32[16,11,64,64]{3,2,0,1:T(8,128)} %reshape.61, f32[16,11,64,32]{3,2,1,0:T(8,128)} %reshape.246), kind=kOutput, calls=%fused_computation.22 | convolution fusion | flops 276824064 | bytes 4456448 | tf_op jit(solution)/shard_map/fkab,fkbr->far/dot_general | solution.py:29
  94.9 4.5 %collective-permute-start.10 = (f32[4,2048]{1,0:T(4,128)S(1)}, f32[4,2048]{1,0:T(4,128)S(1)}, u32[]{:S(2)}, u32[]{:S(2)}) collective-permute-start(f32[4,2048]{1,0:T(4,128)S(1)} %broadcast_select_fusion.4), channel_id=1, source_target_pairs={{0,1},{1,2},{2,3},{3,4},{4,5},{5,6},{6,7},{8,9},{9,10},{10,11},{11... | collective-permute-start | bytes 98312 | tf_op jit(solution)/shard_map/ppermute | solution.py:15
  99.5 1.9 collective-permute-start.11
  102.9 4.8 %collective-permute-start.8 = (f32[4,2048]{1,0:T(4,128)S(1)}, f32[4,2048]{1,0:T(4,128)S(1)}, u32[]{:S(2)}, u32[]{:S(2)}) collective-permute-start(f32[4,2048]{1,0:T(4,128)S(1)} %broadcast_select_fusion.6), channel_id=1, source_target_pairs={{0,8},{8,16},{16,24},{24,32},{32,40},{40,48},{48,56},{56,64},{64,7... | collective-permute-start | bytes 98312 | tf_op jit(solution)/shard_map/ppermute | solution.py:15
  109.7 1.6 reshape.241
  111.3 3.2 broadcast_select_fusion
  114.6 5.2 %reshape.247 = f32[16,11,64,32]{3,2,1,0:T(8,128)} reshape(f32[16,11,2048]{2,1,0:T(8,128)} %broadcast_select_fusion) | data formatting | bytes 2883584 | tf_op jit(solution)/shard_map/reshape | solution.py:28
  119.7 12.3 %fusion.12 = f32[16,64,32]{1,2,0:T(8,128)S(1)} fusion(f32[16,11,64,64]{3,2,0,1:T(8,128)} %reshape.61, f32[16,11,64,32]{3,2,1,0:T(8,128)} %reshape.247), kind=kOutput, calls=%fused_computation.23 | convolution fusion | flops 276824064 | bytes 4456448 | tf_op jit(solution)/shard_map/fkab,fkbr->far/dot_general | solution.py:29
  132.7 1.6 fusion.37
  134.4 250.2 %all-reduce.2.cloned.1.call-done = f32[128,128]{1,0:T(8,128)} async-done(((f32[128,128]{1,0:T(8,128)}), f32[128,128]{1,0:T(8,128)}) %all-reduce.2.cloned.1.call-update) | async-done | bytes 65552 | tf_op jit(solution)/shard_map/psum | solution.py:66
  385.9 8.8 %cholesky.16 = f32[96,96]{1,0:T(8,128)S(1)} custom-call(f32[96,96]{1,0:T(8,128)S(1)} %fusion.29), custom_call_target="Cholesky" | custom-call | tf_op jit(solution)/shard_map/jit(cholesky)/cholesky | solution.py:44
  396.1 7.4 %custom-call.10 = f32[1,96,96]{1,2,0:T(8,128)S(1)} custom-call(f32[1,96,96]{2,1,0:T(8,128)S(1)} %fusion.24), custom_call_target="InvertDiagBlocksLowerTriangular" | custom-call | tf_op jit(solution)/shard_map/jit(_cho_solve)/triangular_solve | solution.py:45
  (75 shorter events, 23.6 us)
Async XLA Ops:
  7.2 377.4 %all-reduce.2.cloned.1.call-start = ((), (), s32[]{:S(2)}) async-start(), calls=%async_computation | async-start | bytes 131072 | tf_op jit(solution)/shard_map/psum | solution.py:66
  9.6 23.2 %collective-permute-start = (f32[4,2048]{1,0:T(4,128)S(1)}, f32[4,2048]{1,0:T(4,128)S(1)}, u32[]{:S(2)}, u32[]{:S(2)}) collective-permute-start(f32[4,2048]{1,0:T(4,128)S(1)} %broadcast_select_fusion.14), channel_id=1, source_target_pairs={{0,8},{8,16},{16,24},{24,32},{32,40},{40,48},{48,56},{56,64},{64,7... | collective-permute-start | bytes 98312 | tf_op jit(solution)/shard_map/ppermute | solution.py:15
  15.2 17.6 %collective-permute-start.1 = (f32[4,2048]{1,0:T(4,128)S(1)}, f32[4,2048]{1,0:T(4,128)S(1)}, u32[]{:S(2)}, u32[]{:S(2)}) collective-permute-start(f32[4,2048]{1,0:T(4,128)S(1)} %broadcast_select_fusion.13), channel_id=1, source_target_pairs={{8,0},{16,8},{24,16},{32,24},{40,32},{48,40},{56,48},{64,56},{72,6... | collective-permute-start | bytes 98312 | tf_op jit(solution)/shard_map/ppermute | solution.py:15
  18.0 14.8 %collective-permute-start.2 = (f32[4,2048]{1,0:T(4,128)S(1)}, f32[4,2048]{1,0:T(4,128)S(1)}, u32[]{:S(2)}, u32[]{:S(2)}) collective-permute-start(f32[4,2048]{1,0:T(4,128)S(1)} %broadcast_select_fusion.12), channel_id=1, source_target_pairs={{0,1},{1,2},{2,3},{3,4},{4,5},{5,6},{6,7},{8,9},{9,10},{10,11},{11... | collective-permute-start | bytes 98312 | tf_op jit(solution)/shard_map/ppermute | solution.py:15
  23.7 9.2 %collective-permute-start.3 = (f32[4,2048]{1,0:T(4,128)S(1)}, f32[4,2048]{1,0:T(4,128)S(1)}, u32[]{:S(2)}, u32[]{:S(2)}) collective-permute-start(f32[4,2048]{1,0:T(4,128)S(1)} %broadcast_select_fusion.11), channel_id=1, source_target_pairs={{1,0},{2,1},{3,2},{4,3},{5,4},{6,5},{7,6},{9,8},{10,9},{11,10},{12... | collective-permute-start | bytes 98312 | tf_op jit(solution)/shard_map/ppermute | solution.py:15
  27.1 5.7 %copy-start = (f32[16,2048]{1,0:T(8,128)S(1)}, f32[16,2048]{1,0:T(8,128)}, u32[]{:S(2)}) copy-start(f32[16,2048]{1,0:T(8,128)} %param.8) | copy-start | bytes 393220
  55.8 12.2 %collective-permute-start.5 = (f32[4,2048]{1,0:T(4,128)S(1)}, f32[4,2048]{1,0:T(4,128)S(1)}, u32[]{:S(2)}, u32[]{:S(2)}) collective-permute-start(f32[4,2048]{1,0:T(4,128)S(1)} %broadcast_select_fusion.9), channel_id=1, source_target_pairs={{8,0},{16,8},{24,16},{32,24},{40,32},{48,40},{56,48},{64,56},{72,6... | collective-permute-start | bytes 98312 | tf_op jit(solution)/shard_map/ppermute | solution.py:15
  57.2 10.8 %collective-permute-start.6 = (f32[4,2048]{1,0:T(4,128)S(1)}, f32[4,2048]{1,0:T(4,128)S(1)}, u32[]{:S(2)}, u32[]{:S(2)}) collective-permute-start(f32[4,2048]{1,0:T(4,128)S(1)} %broadcast_select_fusion.8), channel_id=1, source_target_pairs={{0,1},{1,2},{2,3},{3,4},{4,5},{5,6},{6,7},{8,9},{9,10},{10,11},{11... | collective-permute-start | bytes 98312 | tf_op jit(solution)/shard_map/ppermute | solution.py:15
  60.9 7.1 %collective-permute-start.7 = (f32[4,2048]{1,0:T(4,128)S(1)}, f32[4,2048]{1,0:T(4,128)S(1)}, u32[]{:S(2)}, u32[]{:S(2)}) collective-permute-start(f32[4,2048]{1,0:T(4,128)S(1)} %broadcast_select_fusion.7), channel_id=1, source_target_pairs={{1,0},{2,1},{3,2},{4,3},{5,4},{6,5},{7,6},{9,8},{10,9},{11,10},{12... | collective-permute-start | bytes 98312 | tf_op jit(solution)/shard_map/ppermute | solution.py:15
  62.9 5.9 %collective-permute-start.4 = (f32[4,2048]{1,0:T(4,128)S(1)}, f32[4,2048]{1,0:T(4,128)S(1)}, u32[]{:S(2)}, u32[]{:S(2)}) collective-permute-start(f32[4,2048]{1,0:T(4,128)S(1)} %broadcast_select_fusion.10), channel_id=1, source_target_pairs={{0,8},{8,16},{16,24},{24,32},{32,40},{40,48},{48,56},{56,64},{64,7... | collective-permute-start | bytes 98312 | tf_op jit(solution)/shard_map/ppermute | solution.py:15
  94.9 12.9 %collective-permute-start.10 = (f32[4,2048]{1,0:T(4,128)S(1)}, f32[4,2048]{1,0:T(4,128)S(1)}, u32[]{:S(2)}, u32[]{:S(2)}) collective-permute-start(f32[4,2048]{1,0:T(4,128)S(1)} %broadcast_select_fusion.4), channel_id=1, source_target_pairs={{0,1},{1,2},{2,3},{3,4},{4,5},{5,6},{6,7},{8,9},{9,10},{10,11},{11... | collective-permute-start | bytes 98312 | tf_op jit(solution)/shard_map/ppermute | solution.py:15
  99.5 8.3 %collective-permute-start.11 = (f32[4,2048]{1,0:T(4,128)S(1)}, f32[4,2048]{1,0:T(4,128)S(1)}, u32[]{:S(2)}, u32[]{:S(2)}) collective-permute-start(f32[4,2048]{1,0:T(4,128)S(1)} %broadcast_select_fusion.3), channel_id=1, source_target_pairs={{1,0},{2,1},{3,2},{4,3},{5,4},{6,5},{7,6},{9,8},{10,9},{11,10},{12... | collective-permute-start | bytes 98312 | tf_op jit(solution)/shard_map/ppermute | solution.py:15
  101.5 6.3 %collective-permute-start.9 = (f32[4,2048]{1,0:T(4,128)S(1)}, f32[4,2048]{1,0:T(4,128)S(1)}, u32[]{:S(2)}, u32[]{:S(2)}) collective-permute-start(f32[4,2048]{1,0:T(4,128)S(1)} %broadcast_select_fusion.5), channel_id=1, source_target_pairs={{8,0},{16,8},{24,16},{32,24},{40,32},{48,40},{56,48},{64,56},{72,6... | collective-permute-start | bytes 98312 | tf_op jit(solution)/shard_map/ppermute | solution.py:15
  102.9 5.6 %collective-permute-start.8 = (f32[4,2048]{1,0:T(4,128)S(1)}, f32[4,2048]{1,0:T(4,128)S(1)}, u32[]{:S(2)}, u32[]{:S(2)}) collective-permute-start(f32[4,2048]{1,0:T(4,128)S(1)} %broadcast_select_fusion.6), channel_id=1, source_target_pairs={{0,8},{8,16},{16,24},{24,32},{32,40},{40,48},{48,56},{56,64},{64,7... | collective-permute-start | bytes 98312 | tf_op jit(solution)/shard_map/ppermute | solution.py:15
Sparse Core Ops, SparseCore 0:
  134.5 250.0 all-reduce.1
where the time goes:
time: 416 us; the launch traced here: 415 us
  waiting for transfers between devices  252 us (61%)
  matrix products  42.2 us (10%)
  local copies, waits for them, and re-layouts  41.9 us (10%)
  starting transfers between devices  35.5 us (9%)
  other arithmetic  29.4 us (7%)
  between operations  14.5 us (3%)
    psum x1, waiting for transfers between devices, on_device(): gram_total = lax.psum(local_gram, ('fx', 'fy'))  250 us
    dot_general x3, matrix products, contract(): jnp.einsum('fkab,fkbr->far', block_mats, shaped, precision=lax.Precision....  36.3 us
    ppermute x12, starting transfers between devices, from_behind(): return lax.ppermute(block, axis, route)  35.5 us
    reshape x3, local copies, waits for them, and re-layouts, contract(): shaped = picked.reshape(face_count, picked.shape[1], DOF, NRHS)  13.9 us
    another operation x3, other arithmetic, solve_small(): factor = jnp.linalg.cholesky(normal_matrix)  9.45 us
    select_n x4, other arithmetic, on_device(): jnp.take(extended, face_columns, axis=0)  8.94 us
  transfers between devices with their start and end apart: 13, of which 3 were waited for; matrix products, arithmetic and copies ran while one was open for 3% of the time, Pallas kernels for 0%

commit v1 on v0

--- a/solution.py
+++ b/solution.py
@@ -2,6 +2,7 @@
 import jax.numpy as jnp
 from jax import lax
 from jax.sharding import PartitionSpec as P
+from jax.lax import all_gather
 
 DOF = 64
 NRHS = 32
@@ -63,7 +64,7 @@
         fields.append(contract(block_mats, jnp.take(extended, face_columns, axis=0)))
     stacked = jnp.concatenate([as_rows(item) for item in fields], axis=1)
     local_gram = jnp.dot(stacked.T, stacked, precision=high, preferred_element_type=jnp.float32)
-    gram_total = lax.psum(local_gram, ("fx", "fy"))
+    gram_total = jnp.sum(all_gather(local_gram, ("fx", "fy")), 0)
     coeffs, combo = solve_small(gram_total)
     solution = jnp.dot(stacked[:, : POWERS * NRHS], coeffs, precision=high)
     residual = jnp.dot(stacked, combo, precision=high)

time: 416 us -> 308 us (0.74)
  waiting for transfers between devices: 252 us -> 139 us
  other arithmetic: 29.4 us -> 36 us
    psum x1 -> x0, waiting for transfers between devices: 250 us -> none  [on_device(): gram_total = lax.psum(local_gram, ('fx', 'fy'))]
    all_gather x0 -> x1, waiting for transfers between devices: none -> 137 us  [on_device(): gram_total = jnp.sum(all_gather(local_gram, ('fx', 'fy')), 0)]
    reduce_sum x0 -> x1, other arithmetic: none -> 6.59 us  [on_device(): gram_total = jnp.sum(all_gather(local_gram, ('fx', 'fy')), 0)]
  transfers between devices with their start and end apart: 13 -> 13, of which waited for: 3 -> 3; matrix products, arithmetic and copies ran while one was open for 3% -> 4% of each run, Pallas kernels for 0% -> 0%
where the time goes in v1:
time: 308 us; the launch traced here: 307 us
  waiting for transfers between devices  139 us (45%)
  local copies, waits for them, and re-layouts  41.9 us (14%)
  matrix products  40.5 us (13%)
  other arithmetic  36 us (12%)
  starting transfers between devices  35.5 us (12%)
  between operations  14.5 us (5%)
    all_gather x1, waiting for transfers between devices, on_device(): gram_total = jnp.sum(all_gather(local_gram, ('fx', 'fy')), 0)  137 us
    dot_general x3, matrix products, contract(): jnp.einsum('fkab,fkbr->far', block_mats, shaped, precision=lax.Precision....  36.3 us
    ppermute x12, starting transfers between devices, from_behind(): return lax.ppermute(block, axis, route)  35.5 us
    reshape x3, local copies, waits for them, and re-layouts, contract(): shaped = picked.reshape(face_count, picked.shape[1], DOF, NRHS)  13.9 us
    another operation x3, other arithmetic, solve_small(): factor = jnp.linalg.cholesky(normal_matrix)  9.45 us
    select_n x4, other arithmetic, on_device(): jnp.take(extended, face_columns, axis=0)  8.94 us
    gather x6, local copies, waits for them, and re-layouts, on_device(): jnp.take(extended, face_columns, axis=0)  8.28 us
    another operation x2, other arithmetic, solve_small(): coeffs = jax.scipy.linalg.cho_solve((factor, True), right_terms)  8.01 us
  transfers between devices with their start and end apart: 13, of which 3 were waited for; matrix products, arithmetic and copies ran while one was open for 4% of the time, Pallas kernels for 0%

profile of v1, /device:TPU:1, one launch (start us, length us, event | category | flops | bytes accessed | tf_op | source)
XLA Modules:
  0.0 307.3 jit_solution(12428041236761834593)
XLA Ops:
  8.1 1.5 gather_fusion
  9.6 3.9 %collective-permute-start = (f32[4,2048]{1,0:T(4,128)S(1)}, f32[4,2048]{1,0:T(4,128)S(1)}, u32[]{:S(2)}, u32[]{:S(2)}) collective-permute-start(f32[4,2048]{1,0:T(4,128)S(1)} %broadcast_select_fusion.14), channel_id=1, source_target_pairs={{0,8},{8,16},{16,24},{24,32},{32,40},{40,48},{48,56},{56,64},{64,7... | collective-permute-start | bytes 98312 | tf_op jit(solution)/shard_map/ppermute | solution.py:16
  13.6 1.5 gather_fusion.1
  15.2 1.3 collective-permute-start.1
  16.5 1.5 gather_fusion.2
  18.0 4.0 %collective-permute-start.2 = (f32[4,2048]{1,0:T(4,128)S(1)}, f32[4,2048]{1,0:T(4,128)S(1)}, u32[]{:S(2)}, u32[]{:S(2)}) collective-permute-start(f32[4,2048]{1,0:T(4,128)S(1)} %broadcast_select_fusion.12), channel_id=1, source_target_pairs={{0,1},{1,2},{2,3},{3,4},{4,5},{5,6},{6,7},{8,9},{9,10},{10,11},{11... | collective-permute-start | bytes 98312 | tf_op jit(solution)/shard_map/ppermute | solution.py:16
  22.1 1.5 gather_fusion.3
  23.7 1.9 collective-permute-start.3
  27.1 5.7 %reshape.61 = f32[16,11,64,64]{3,2,0,1:T(8,128)} reshape(f32[16,11,4096]{2,0,1:T(8,128)} %param.9) | data formatting | bytes 5767168 | tf_op jit(solution)/shard_map/reshape | solution.py:53
  34.1 1.5 reshape.218
  35.6 1.8 broadcast_select_fusion.2
  37.4 3.6 %reshape.246 = f32[16,11,64,32]{3,2,1,0:T(8,128)} reshape(f32[16,11,2048]{2,1,0:T(8,128)S(1)} %broadcast_select_fusion.2) | data formatting | bytes 2883584 | tf_op jit(solution)/shard_map/reshape | solution.py:29
  41.0 12.0 %fusion.6 = f32[16,64,32]{1,2,0:T(8,128)S(1)} fusion(f32[16,11,64,64]{3,2,0,1:T(8,128)} %reshape.61, f32[16,11,64,32]{3,2,1,0:T(8,128)} %reshape.246), kind=kOutput, calls=%fused_computation.21 | convolution fusion | flops 276824064 | bytes 4456448 | tf_op jit(solution)/shard_map/fkab,fkbr->far/dot_general | solution.py:30
  57.2 3.6 %collective-permute-start.6 = (f32[4,2048]{1,0:T(4,128)S(1)}, f32[4,2048]{1,0:T(4,128)S(1)}, u32[]{:S(2)}, u32[]{:S(2)}) collective-permute-start(f32[4,2048]{1,0:T(4,128)S(1)} %broadcast_select_fusion.8), channel_id=1, source_target_pairs={{0,1},{1,2},{2,3},{3,4},{4,5},{5,6},{6,7},{8,9},{9,10},{10,11},{11... | collective-permute-start | bytes 98312 | tf_op jit(solution)/shard_map/ppermute | solution.py:16
  60.9 1.9 collective-permute-start.7
  62.9 5.1 %collective-permute-start.4 = (f32[4,2048]{1,0:T(4,128)S(1)}, f32[4,2048]{1,0:T(4,128)S(1)}, u32[]{:S(2)}, u32[]{:S(2)}) collective-permute-start(f32[4,2048]{1,0:T(4,128)S(1)} %broadcast_select_fusion.10), channel_id=1, source_target_pairs={{0,8},{8,16},{16,24},{24,32},{32,40},{40,48},{48,56},{56,64},{64,7... | collective-permute-start | bytes 98312 | tf_op jit(solution)/shard_map/ppermute | solution.py:16
  70.0 1.6 reshape.230
  71.7 3.2 %broadcast_select_fusion.1 = f32[16,11,2048]{2,1,0:T(8,128)} fusion(f32[16,11,2048]{2,1,0:T(8,128)} %reshape.230, pred[16,11]{1,0:T(8,128)(4,1)S(1)} %compare_and_fusion), kind=kLoop, calls=%fused_computation.26 | loop fusion | flops 360448 | bytes 2883760 | tf_op jit(solution)/shard_map/jit(_take)/select_n | solution.py:64
  74.9 5.2 %reshape.247 = f32[16,11,64,32]{3,2,1,0:T(8,128)} reshape(f32[16,11,2048]{2,1,0:T(8,128)} %broadcast_select_fusion.1) | data formatting | bytes 2883584 | tf_op jit(solution)/shard_map/reshape | solution.py:29
  80.1 12.0 %fusion.9 = f32[16,64,32]{1,2,0:T(8,128)S(1)} fusion(f32[16,11,64,64]{3,2,0,1:T(8,128)} %reshape.61, f32[16,11,64,32]{3,2,1,0:T(8,128)} %reshape.247), kind=kOutput, calls=%fused_computation.22 | convolution fusion | flops 276824064 | bytes 4456448 | tf_op jit(solution)/shard_map/fkab,fkbr->far/dot_general | solution.py:30
  94.9 4.5 %collective-permute-start.10 = (f32[4,2048]{1,0:T(4,128)S(1)}, f32[4,2048]{1,0:T(4,128)S(1)}, u32[]{:S(2)}, u32[]{:S(2)}) collective-permute-start(f32[4,2048]{1,0:T(4,128)S(1)} %broadcast_select_fusion.4), channel_id=1, source_target_pairs={{0,1},{1,2},{2,3},{3,4},{4,5},{5,6},{6,7},{8,9},{9,10},{10,11},{11... | collective-permute-start | bytes 98312 | tf_op jit(solution)/shard_map/ppermute | solution.py:16
  99.5 1.9 collective-permute-start.11
  102.9 4.8 %collective-permute-start.8 = (f32[4,2048]{1,0:T(4,128)S(1)}, f32[4,2048]{1,0:T(4,128)S(1)}, u32[]{:S(2)}, u32[]{:S(2)}) collective-permute-start(f32[4,2048]{1,0:T(4,128)S(1)} %broadcast_select_fusion.6), channel_id=1, source_target_pairs={{0,8},{8,16},{16,24},{24,32},{32,40},{40,48},{48,56},{56,64},{64,7... | collective-permute-start | bytes 98312 | tf_op jit(solution)/shard_map/ppermute | solution.py:16
  109.7 1.6 reshape.242
  111.3 3.2 %broadcast_select_fusion = f32[16,11,2048]{2,1,0:T(8,128)} fusion(f32[16,11,2048]{2,1,0:T(8,128)} %reshape.242, pred[16,11]{1,0:T(8,128)(4,1)S(1)} %compare_and_fusion), kind=kLoop, calls=%fused_computation.25 | loop fusion | flops 360448 | bytes 2883760 | tf_op jit(solution)/shard_map/jit(_take)/select_n | solution.py:64
  114.6 5.2 %reshape.248 = f32[16,11,64,32]{3,2,1,0:T(8,128)} reshape(f32[16,11,2048]{2,1,0:T(8,128)} %broadcast_select_fusion) | data formatting | bytes 2883584 | tf_op jit(solution)/shard_map/reshape | solution.py:29
  119.7 12.3 %fusion.12 = f32[16,64,32]{1,2,0:T(8,128)S(1)} fusion(f32[16,11,64,64]{3,2,0,1:T(8,128)} %reshape.61, f32[16,11,64,32]{3,2,1,0:T(8,128)} %reshape.248), kind=kOutput, calls=%fused_computation.23 | convolution fusion | flops 276824064 | bytes 4456448 | tf_op jit(solution)/shard_map/fkab,fkbr->far/dot_general | solution.py:30
  132.7 1.6 fusion.37
  134.4 137.5 %all-gather.3.cloned.1.call-done = f32[32768,128]{1,0:T(8,128)} async-done(((f32[128,128]{1,0:T(8,128)}), f32[32768,128]{1,0:T(8,128)}) %all-gather.3.cloned.1.call-update) | async-done | bytes 16777232 | tf_op jit(solution)/shard_map/all_gather | solution.py:67
  271.9 6.6 %reduce_sum.9 = f32[128,128]{1,0:T(8,128)S(1)} reduce(f32[256,128,128]{2,1,0:T(8,128)} %bitcast.54, f32[]{:T(128)} %constant.68.clone.1), dimensions={0}, to_apply=%region_0.3 | reduce | flops 4177920 | bytes 16842756 | tf_op jit(solution)/shard_map/reduce_sum | solution.py:67
  279.2 8.8 %cholesky.16 = f32[96,96]{1,0:T(8,128)S(1)} custom-call(f32[96,96]{1,0:T(8,128)S(1)} %fusion.29), custom_call_target="Cholesky" | custom-call | tf_op jit(solution)/shard_map/jit(cholesky)/cholesky | solution.py:45
  289.3 7.4 %custom-call.10 = f32[1,96,96]{1,2,0:T(8,128)S(1)} custom-call(f32[1,96,96]{2,1,0:T(8,128)S(1)} %fusion.24), custom_call_target="InvertDiagBlocksLowerTriangular" | custom-call | tf_op jit(solution)/shard_map/jit(_cho_solve)/triangular_solve | solution.py:46
  (76 shorter events, 23.2 us)
Async XLA Ops:
  7.2 264.7 %all-gather.3.cloned.1.call-start = ((), (), s32[]{:S(2)}) async-start(), calls=%async_computation | async-start | bytes 16842752 | tf_op jit(solution)/shard_map/all_gather | solution.py:67
  9.6 23.2 %collective-permute-start = (f32[4,2048]{1,0:T(4,128)S(1)}, f32[4,2048]{1,0:T(4,128)S(1)}, u32[]{:S(2)}, u32[]{:S(2)}) collective-permute-start(f32[4,2048]{1,0:T(4,128)S(1)} %broadcast_select_fusion.14), channel_id=1, source_target_pairs={{0,8},{8,16},{16,24},{24,32},{32,40},{40,48},{48,56},{56,64},{64,7... | collective-permute-start | bytes 98312 | tf_op jit(solution)/shard_map/ppermute | solution.py:16
  15.2 17.6 %collective-permute-start.1 = (f32[4,2048]{1,0:T(4,128)S(1)}, f32[4,2048]{1,0:T(4,128)S(1)}, u32[]{:S(2)}, u32[]{:S(2)}) collective-permute-start(f32[4,2048]{1,0:T(4,128)S(1)} %broadcast_select_fusion.13), channel_id=1, source_target_pairs={{8,0},{16,8},{24,16},{32,24},{40,32},{48,40},{56,48},{64,56},{72,6... | collective-permute-start | bytes 98312 | tf_op jit(solution)/shard_map/ppermute | solution.py:16
  18.0 14.8 %collective-permute-start.2 = (f32[4,2048]{1,0:T(4,128)S(1)}, f32[4,2048]{1,0:T(4,128)S(1)}, u32[]{:S(2)}, u32[]{:S(2)}) collective-permute-start(f32[4,2048]{1,0:T(4,128)S(1)} %broadcast_select_fusion.12), channel_id=1, source_target_pairs={{0,1},{1,2},{2,3},{3,4},{4,5},{5,6},{6,7},{8,9},{9,10},{10,11},{11... | collective-permute-start | bytes 98312 | tf_op jit(solution)/shard_map/ppermute | solution.py:16
  23.7 9.2 %collective-permute-start.3 = (f32[4,2048]{1,0:T(4,128)S(1)}, f32[4,2048]{1,0:T(4,128)S(1)}, u32[]{:S(2)}, u32[]{:S(2)}) collective-permute-start(f32[4,2048]{1,0:T(4,128)S(1)} %broadcast_select_fusion.11), channel_id=1, source_target_pairs={{1,0},{2,1},{3,2},{4,3},{5,4},{6,5},{7,6},{9,8},{10,9},{11,10},{12... | collective-permute-start | bytes 98312 | tf_op jit(solution)/shard_map/ppermute | solution.py:16
  27.1 5.7 %copy-start = (f32[16,2048]{1,0:T(8,128)S(1)}, f32[16,2048]{1,0:T(8,128)}, u32[]{:S(2)}) copy-start(f32[16,2048]{1,0:T(8,128)} %param.8) | copy-start | bytes 393220
  55.8 12.2 %collective-permute-start.5 = (f32[4,2048]{1,0:T(4,128)S(1)}, f32[4,2048]{1,0:T(4,128)S(1)}, u32[]{:S(2)}, u32[]{:S(2)}) collective-permute-start(f32[4,2048]{1,0:T(4,128)S(1)} %broadcast_select_fusion.9), channel_id=1, source_target_pairs={{8,0},{16,8},{24,16},{32,24},{40,32},{48,40},{56,48},{64,56},{72,6... | collective-permute-start | bytes 98312 | tf_op jit(solution)/shard_map/ppermute | solution.py:16
  57.2 10.8 %collective-permute-start.6 = (f32[4,2048]{1,0:T(4,128)S(1)}, f32[4,2048]{1,0:T(4,128)S(1)}, u32[]{:S(2)}, u32[]{:S(2)}) collective-permute-start(f32[4,2048]{1,0:T(4,128)S(1)} %broadcast_select_fusion.8), channel_id=1, source_target_pairs={{0,1},{1,2},{2,3},{3,4},{4,5},{5,6},{6,7},{8,9},{9,10},{10,11},{11... | collective-permute-start | bytes 98312 | tf_op jit(solution)/shard_map/ppermute | solution.py:16
  60.9 7.1 %collective-permute-start.7 = (f32[4,2048]{1,0:T(4,128)S(1)}, f32[4,2048]{1,0:T(4,128)S(1)}, u32[]{:S(2)}, u32[]{:S(2)}) collective-permute-start(f32[4,2048]{1,0:T(4,128)S(1)} %broadcast_select_fusion.7), channel_id=1, source_target_pairs={{1,0},{2,1},{3,2},{4,3},{5,4},{6,5},{7,6},{9,8},{10,9},{11,10},{12... | collective-permute-start | bytes 98312 | tf_op jit(solution)/shard_map/ppermute | solution.py:16
  62.9 5.9 %collective-permute-start.4 = (f32[4,2048]{1,0:T(4,128)S(1)}, f32[4,2048]{1,0:T(4,128)S(1)}, u32[]{:S(2)}, u32[]{:S(2)}) collective-permute-start(f32[4,2048]{1,0:T(4,128)S(1)} %broadcast_select_fusion.10), channel_id=1, source_target_pairs={{0,8},{8,16},{16,24},{24,32},{32,40},{40,48},{48,56},{56,64},{64,7... | collective-permute-start | bytes 98312 | tf_op jit(solution)/shard_map/ppermute | solution.py:16
  94.9 12.9 %collective-permute-start.10 = (f32[4,2048]{1,0:T(4,128)S(1)}, f32[4,2048]{1,0:T(4,128)S(1)}, u32[]{:S(2)}, u32[]{:S(2)}) collective-permute-start(f32[4,2048]{1,0:T(4,128)S(1)} %broadcast_select_fusion.4), channel_id=1, source_target_pairs={{0,1},{1,2},{2,3},{3,4},{4,5},{5,6},{6,7},{8,9},{9,10},{10,11},{11... | collective-permute-start | bytes 98312 | tf_op jit(solution)/shard_map/ppermute | solution.py:16
  99.5 8.3 %collective-permute-start.11 = (f32[4,2048]{1,0:T(4,128)S(1)}, f32[4,2048]{1,0:T(4,128)S(1)}, u32[]{:S(2)}, u32[]{:S(2)}) collective-permute-start(f32[4,2048]{1,0:T(4,128)S(1)} %broadcast_select_fusion.3), channel_id=1, source_target_pairs={{1,0},{2,1},{3,2},{4,3},{5,4},{6,5},{7,6},{9,8},{10,9},{11,10},{12... | collective-permute-start | bytes 98312 | tf_op jit(solution)/shard_map/ppermute | solution.py:16
  101.5 6.3 %collective-permute-start.9 = (f32[4,2048]{1,0:T(4,128)S(1)}, f32[4,2048]{1,0:T(4,128)S(1)}, u32[]{:S(2)}, u32[]{:S(2)}) collective-permute-start(f32[4,2048]{1,0:T(4,128)S(1)} %broadcast_select_fusion.5), channel_id=1, source_target_pairs={{8,0},{16,8},{24,16},{32,24},{40,32},{48,40},{56,48},{64,56},{72,6... | collective-permute-start | bytes 98312 | tf_op jit(solution)/shard_map/ppermute | solution.py:16
  102.9 5.6 %collective-permute-start.8 = (f32[4,2048]{1,0:T(4,128)S(1)}, f32[4,2048]{1,0:T(4,128)S(1)}, u32[]{:S(2)}, u32[]{:S(2)}) collective-permute-start(f32[4,2048]{1,0:T(4,128)S(1)} %broadcast_select_fusion.6), channel_id=1, source_target_pairs={{0,8},{8,16},{16,24},{24,32},{32,40},{40,48},{48,56},{56,64},{64,7... | collective-permute-start | bytes 98312 | tf_op jit(solution)/shard_map/ppermute | solution.py:16
Sparse Core Ops, SparseCore 0:
  134.5 137.3 all-gather.2
